TPU v7x, 512 devices: a whole 4x8x8 slice. The times are simulated.
512 devices in a mesh: panel: 2 (over z_hi), colat: 16 (over z_lo, x), lon: 16 (over y, core).
Axes of the slice: x: 4, y: 8, z: 8 (z_hi: 2, z_lo: 4; z = z_hi * 4 + z_lo), core: 2. Of those that a mesh axis runs over, the one named last changes fastest.
Arguments:
- fields_now: float32 [4, 2, 256, 512, 128], P(None, 'panel', 'colat', 'lon'), may hold values from -6 to 6
- diffusivity: float32 [2, 256, 512, 128], P('panel', 'colat', 'lon'), may hold values from 0.5 to 2
- viscosity: float32 [2, 256, 512, 128], P('panel', 'colat', 'lon'), may hold values from 0.5 to 2
- donor_row: int32 [2, 16, 16, 12], P('panel', 'colat', 'lon'), may hold values from 0 to 16
- donor_column: int32 [2, 16, 16, 12], P('panel', 'colat', 'lon'), may hold values from 0 to 32
- donor_offset: float32 [2, 16, 16, 2, 12], P('panel', 'colat', 'lon'), may hold values from 0 to 1
- rim_angle: float32 [2, 16, 16, 12], P('panel', 'colat', 'lon'), may hold values from -3.140625 to 3.140625
Outputs:
- advanced: float32 [4, 2, 256, 512, 128], P(None, 'panel', 'colat', 'lon')
All inputs are finite; a program needn't handle non-finite values.
Results may differ from a plain program's by a relative error of at most 0.00002.
Values sent between devices are 32-bit elements; how exact they have to be, the bound alone decides.
A program may use at most 64 MiB of HBM per device.

v0:
```python
import jax
import jax.numpy as jnp
from jax import lax
from jax.sharding import PartitionSpec as P

TIME_STEP = 0.05
BUOYANCY = 1.0


def with_halo(x, sides, width):
    for axis, dim in sides:
        count, length = (lax.axis_size(axis), x.shape[dim])
        up = [(i, (i + 1) % count) for i in range(count - 1)]
        down = [(j, i) for i, j in up]
        last = lax.slice_in_dim(x, length - width, length, axis=dim)
        leading = lax.slice_in_dim(x, 0, width, axis=dim)
        before = lax.ppermute(last, axis, up)
        after = lax.ppermute(leading, axis, down)
        x = jnp.concatenate([before, x, after], axis=dim)
    return x


def swapped(block, axis, stride):
    count = lax.axis_size(axis)
    route = []
    for low in range(count):
        high = low | 1 << stride
        if high != low and high < count:
            route += [(low, high), (high, low)]
    return lax.ppermute(block, axis, route)


def gradient(stencil):
    return (8.0 * (stencil[3] - stencil[1]) - (stencil[4] - stencil[0])) / 12.0


def curvature(stencil):
    return (16.0 * (stencil[3] + stencil[1]) - (stencil[4] + stencil[0]) - 30.0 * stencil[2]) / 12.0


def advance(padded, thermal, viscous):
    height = padded.shape[1] - 4
    breadth = padded.shape[2] - 4
    center = padded[:, 2 : 2 + height, 2 : 2 + breadth]
    radial_len = center.shape[3]
    radial_pad = jnp.pad(center, ((0, 0), (0, 0), (0, 0), (2, 2)))
    along_lat = [padded[:, offset : offset + height, 2 : 2 + breadth] for offset in range(5)]
    along_lon = [padded[:, 2 : 2 + height, offset : offset + breadth] for offset in range(5)]
    along_rad = [radial_pad[..., offset : offset + radial_len] for offset in range(5)]
    laplace = curvature(along_rad) + curvature(along_lat) + curvature(along_lon)
    transport = (
        center[1:2] * gradient(along_rad)
        + center[2:3] * gradient(along_lat)
        + center[3:4] * gradient(along_lon)
    )
    diffusion = jnp.stack([thermal, viscous, viscous, viscous])
    change = diffusion * laplace - transport
    change = change.at[1].add(BUOYANCY * center[0])
    return center + TIME_STEP * change


def local(fields_now, diffusivity, viscosity, donor_row, donor_column, donor_offset, rim_angle):
    fields = fields_now[:, 0]
    thermal = diffusivity[0]
    viscous = viscosity[0]
    height = fields.shape[1]
    breadth = fields.shape[2]
    radial_len = fields.shape[3]
    colat_pos = lax.axis_index("colat")
    lon_pos = lax.axis_index("lon")
    colat_count = lax.axis_size("colat")
    lon_count = lax.axis_size("lon")
    row_share = 4 * breadth // colat_count
    padded = with_halo(fields, (("colat", 1), ("lon", 2)), 2)
    fresh = advance(padded, thermal, viscous)
    extended = with_halo(fresh, (("colat", 1), ("lon", 2)), 1)
    width = breadth + 2
    flattened = extended.reshape(4, (height + 2) * width, radial_len)
    anchor = donor_row.reshape(-1) * width + donor_column.reshape(-1)

    def corner(offset):
        return jnp.take(flattened, anchor + offset, axis=1)

    frac_row = donor_offset[0, 0, 0, 0][None, :, None]
    frac_lon = donor_offset[0, 0, 0, 1][None, :, None]
    blended = (1.0 - frac_row) * (
        (1.0 - frac_lon) * corner(0) + frac_lon * corner(1)
    ) + frac_row * ((1.0 - frac_lon) * corner(width) + frac_lon * corner(width + 1))
    angles = rim_angle.reshape(-1)
    cosine = jnp.cos(angles)[:, None]
    sine_part = jnp.sin(angles)[:, None]
    turned_lat = cosine * blended[2] - sine_part * blended[3]
    turned_lon = sine_part * blended[2] + cosine * blended[3]
    blended = jnp.stack([blended[0], blended[1], turned_lat, turned_lon])
    arrived = swapped(blended, "panel", 0)
    row_full = lax.all_gather(arrived[:, 0:row_share], "colat", axis=1, tiled=True)
    col_full = lax.all_gather(arrived[:, row_share:], "lon", axis=1, tiled=True)
    col_blocks = col_full.reshape(4, 4, height, radial_len)
    west_strip = jnp.transpose(
        jnp.stack([col_blocks[:, 0], col_blocks[:, 2]], axis=1), (0, 2, 1, 3)
    )
    east_strip = jnp.transpose(
        jnp.stack([col_blocks[:, 3], col_blocks[:, 1]], axis=1), (0, 2, 1, 3)
    )
    fresh = fresh.at[:, :, 0:2].set(jnp.where(lon_pos == 0, west_strip, fresh[:, :, 0:2]))
    fresh = fresh.at[:, :, breadth - 2 :].set(
        jnp.where(lon_pos == lon_count - 1, east_strip, fresh[:, :, breadth - 2 :])
    )
    row_blocks = row_full.reshape(4, 4, breadth, radial_len)
    north_strip = jnp.stack([row_blocks[:, 0], row_blocks[:, 2]], axis=1)
    south_strip = jnp.stack([row_blocks[:, 3], row_blocks[:, 1]], axis=1)
    fresh = fresh.at[:, 0:2].set(jnp.where(colat_pos == 0, north_strip, fresh[:, 0:2]))
    fresh = fresh.at[:, height - 2 :].set(
        jnp.where(colat_pos == colat_count - 1, south_strip, fresh[:, height - 2 :])
    )
    return fresh[:, None]


def solution(mesh):
    placed = (
        P(None, "panel", "colat", "lon", None),
        P("panel", "colat", "lon", None),
        P("panel", "colat", "lon", None),
        P("panel", "colat", "lon", None),
        P("panel", "colat", "lon", None),
        P("panel", "colat", "lon", None, None),
        P("panel", "colat", "lon", None),
    )
    return jax.shard_map(
        local,
        mesh=mesh,
        in_specs=placed,
        out_specs=P(None, "panel", "colat", "lon", None),
        check_vma=False,
    )
```

profile of v0, /device:TPU:24, one launch (start us, length us, event | category | flops | bytes accessed | tf_op | source)
XLA Modules:
  0.0 119.8 jit_solution(8745832736168921647)
XLA Ops:
  0.0 1.9 %copy.67 = f32[4,1,16,32,128]{4,2,3,0,1:T(8,128)S(1)} copy(f32[4,1,16,32,128]{4,3,2,1,0:T(8,128)} %param.19) | data formatting | bytes 2097152 | tf_op args[0]
  1.9 0.1 fusion.16
  2.0 1.3 %collective-permute-start = (f32[4,2,32,128]{3,1,2,0:T(2,128)S(1)}, f32[4,2,32,128]{3,1,2,0:T(2,128)S(1)}, u32[]{:S(2)}, u32[]{:S(2)}) collective-permute-start(f32[4,2,32,128]{3,1,2,0:T(2,128)S(1)} %get-tuple-element.87), channel_id=1, source_target_pairs={{16,0},{32,16},{48,32},{64,48},{80,64},{96,80},{112,96},{128,112},... | collective-permute-start | bytes 393224 | tf_op jit(solution)/shard_map/ppermute | solution.py:18
  3.3 0.0 copy-start.1
  3.4 0.0 copy-start.2
  3.4 4.7 %collective-permute-start.1 = (f32[4,2,32,128]{3,1,2,0:T(2,128)S(1)}, f32[4,2,32,128]{3,1,2,0:T(2,128)S(1)}, u32[]{:S(2)}, u32[]{:S(2)}) collective-permute-start(f32[4,2,32,128]{3,1,2,0:T(2,128)S(1)} %get-tuple-element.86), channel_id=1, source_target_pairs={{0,16},{16,32},{32,48},{48,64},{64,80},{80,96},{96,112},{112,128},... | collective-permute-start | bytes 393224 | tf_op jit(solution)/shard_map/ppermute | solution.py:17
  8.1 0.1 fusion.15
  8.3 0.2 copy.42
  8.4 0.2 copy.43
  8.6 0.2 copy.44
  8.8 0.2 copy.38
  9.0 0.2 copy.39
  9.2 1.3 %collective-permute-done.1 = f32[4,2,32,128]{3,1,2,0:T(2,128)S(1)} collective-permute-done((f32[4,2,32,128]{3,1,2,0:T(2,128)S(1)}, f32[4,2,32,128]{3,1,2,0:T(2,128)S(1)}, u32[]{:S(2)}, u32[]{:S(2)}) %collective-permute-start.1) | collective-permute-done | bytes 131104 | tf_op jit(solution)/shard_map/ppermute | solution.py:17
  10.6 1.9 %collective-permute-start.2 = (f32[4,20,2,128]{3,1,2,0:T(8,128)S(1)}, f32[4,20,2,128]{3,1,2,0:T(8,128)S(1)}, u32[]{:S(2)}, u32[]{:S(2)}) collective-permute-start(f32[4,20,2,128]{3,1,2,0:T(8,128)S(1)} %get-tuple-element.76), channel_id=1, source_target_pairs={{1,0},{2,1},{3,2},{4,3},{5,4},{6,5},{7,6},{8,7},{9,8},{10,9},{11,1... | collective-permute-start | bytes 245768 | tf_op jit(solution)/shard_map/ppermute | solution.py:18
  12.5 2.4 %collective-permute-start.3 = (f32[4,20,2,128]{3,1,2,0:T(8,128)S(1)}, f32[4,20,2,128]{3,1,2,0:T(8,128)S(1)}, u32[]{:S(2)}, u32[]{:S(2)}) collective-permute-start(f32[4,20,2,128]{3,1,2,0:T(8,128)S(1)} %get-tuple-element.77), channel_id=1, source_target_pairs={{0,1},{1,2},{2,3},{3,4},{4,5},{5,6},{6,7},{7,8},{8,9},{9,10},{10,1... | collective-permute-start | bytes 245768 | tf_op jit(solution)/shard_map/ppermute | solution.py:17
  15.0 3.5 %collective-permute-done.3 = f32[4,20,2,128]{3,1,2,0:T(8,128)S(1)} collective-permute-done((f32[4,20,2,128]{3,1,2,0:T(8,128)S(1)}, f32[4,20,2,128]{3,1,2,0:T(8,128)S(1)}, u32[]{:S(2)}, u32[]{:S(2)}) %collective-permute-start.3) | collective-permute-done | bytes 81952 | tf_op jit(solution)/shard_map/ppermute | solution.py:17
  18.5 0.3 pad_maximum_fusion
  18.7 2.5 %fusion.2 = f32[4,16,32,128]{3,1,2,0:T(8,128)S(1)} fusion(f32[1,16,32,128]{3,1,2,0:T(8,128)S(1)} %copy.39, f32[1,16,32,128]{3,1,2,0:T(8,128)S(1)} %copy.38, f32[4,20,34,128]{3,1,2,0:T(8,128)S(1)} %get-tuple-element.75, f32[4,20,34,128]{3,1,2,0:T(8,128)S(1)} %get-tuple-element.74, f32[4,2,32,128]{3,1,2,0:T(2,128)S(1)} %collective-permute-done, ...), kind=kLoop, calls=%fused_computation.20 | loop fusion | flops 11796480 | bytes 7864320 | tf_op jit(solution)/shard_map/sub | solution.py:57
  21.2 0.2 fusion.3
  21.5 0.7 multiply_add_fusion
  22.1 0.1 fusion.14
  22.2 4.4 %collective-permute-start.4 = (f32[4,1,32,128]{3,1,2,0:T(1,128)S(1)}, f32[4,1,32,128]{3,1,2,0:T(1,128)S(1)}, u32[]{:S(2)}, u32[]{:S(2)}) collective-permute-start(f32[4,1,32,128]{3,1,2,0:T(1,128)S(1)} %get-tuple-element.80), channel_id=1, source_target_pairs={{0,16},{16,32},{32,48},{48,64},{64,80},{80,96},{96,112},{112,128},... | collective-permute-start | bytes 196616 | tf_op jit(solution)/shard_map/ppermute | solution.py:17
  26.6 1.3 %collective-permute-start.5 = (f32[4,1,32,128]{3,1,2,0:T(1,128)S(1)}, f32[4,1,32,128]{3,1,2,0:T(1,128)S(1)}, u32[]{:S(2)}, u32[]{:S(2)}) collective-permute-start(f32[4,1,32,128]{3,1,2,0:T(1,128)S(1)} %get-tuple-element.81), channel_id=1, source_target_pairs={{16,0},{32,16},{48,32},{64,48},{80,64},{96,80},{112,96},{128,112},... | collective-permute-start | bytes 196616 | tf_op jit(solution)/shard_map/ppermute | solution.py:18
  27.9 0.7 collective-permute-done.4
  28.6 4.2 %collective-permute-done.5 = f32[4,1,32,128]{3,1,2,0:T(1,128)S(1)} collective-permute-done((f32[4,1,32,128]{3,1,2,0:T(1,128)S(1)}, f32[4,1,32,128]{3,1,2,0:T(1,128)S(1)}, u32[]{:S(2)}, u32[]{:S(2)}) %collective-permute-start.5) | collective-permute-done | bytes 65568 | tf_op jit(solution)/shard_map/ppermute | solution.py:18
  32.8 1.9 %collective-permute-start.6 = (f32[4,18,1,128]{3,1,2,0:T(8,128)S(1)}, f32[4,18,1,128]{3,1,2,0:T(8,128)S(1)}, u32[]{:S(2)}, u32[]{:S(2)}) collective-permute-start(f32[4,18,1,128]{3,1,2,0:T(8,128)S(1)} %get-tuple-element.78), channel_id=1, source_target_pairs={{0,1},{1,2},{2,3},{3,4},{4,5},{5,6},{6,7},{7,8},{8,9},{9,10},{10,1... | collective-permute-start | bytes 110600 | tf_op jit(solution)/shard_map/ppermute | solution.py:17
  34.7 3.6 %collective-permute-start.7 = (f32[4,18,1,128]{3,1,2,0:T(8,128)S(1)}, f32[4,18,1,128]{3,1,2,0:T(8,128)S(1)}, u32[]{:S(2)}, u32[]{:S(2)}) collective-permute-start(f32[4,18,1,128]{3,1,2,0:T(8,128)S(1)} %get-tuple-element.79), channel_id=1, source_target_pairs={{1,0},{2,1},{3,2},{4,3},{5,4},{6,5},{7,6},{8,7},{9,8},{10,9},{11,1... | collective-permute-start | bytes 110600 | tf_op jit(solution)/shard_map/ppermute | solution.py:18
  38.4 3.1 %collective-permute-done.7 = f32[4,18,1,128]{3,1,2,0:T(8,128)S(1)} collective-permute-done((f32[4,18,1,128]{3,1,2,0:T(8,128)S(1)}, f32[4,18,1,128]{3,1,2,0:T(8,128)S(1)}, u32[]{:S(2)}, u32[]{:S(2)}) %collective-permute-start.7) | collective-permute-done | bytes 36896 | tf_op jit(solution)/shard_map/ppermute | solution.py:18
  41.4 0.3 pad_maximum_fusion.1
  41.7 0.5 copy.46
  42.2 0.6 gather_fusion.2
  42.8 0.6 gather_fusion.3
  43.4 0.6 gather_fusion.1
  43.9 0.6 gather_fusion
  44.5 0.2 fusion.11
  44.7 0.1 multiply_subtract_fusion
  44.8 10.9 %collective-permute-start.8 = (f32[4,12,128]{2,0,1:T(4,128)S(1)}, f32[4,12,128]{2,0,1:T(4,128)S(1)}, u32[]{:S(2)}, u32[]{:S(2)}) collective-permute-start(f32[4,12,128]{2,0,1:T(4,128)S(1)} %pad_maximum_fusion.10), channel_id=1, source_target_pairs={{0,256},{256,0},{1,257},{257,1},{2,258},{258,2},{3,259},{259,3},{4... | collective-permute-start | bytes 73736 | tf_op jit(solution)/shard_map/ppermute | solution.py:30
  55.8 1.8 %collective-permute-done.8 = f32[4,12,128]{2,0,1:T(4,128)S(1)} collective-permute-done((f32[4,12,128]{2,0,1:T(4,128)S(1)}, f32[4,12,128]{2,0,1:T(4,128)S(1)}, u32[]{:S(2)}, u32[]{:S(2)}) %collective-permute-start.8) | collective-permute-done | bytes 24608 | tf_op jit(solution)/shard_map/ppermute | solution.py:30
  57.6 17.1 %all_gather.6 = f32[4,64,128]{2,0,1:T(4,128)S(1)} all-gather(f32[4,4,128]{2,0,1:T(4,128)S(1)} %slice.349), channel_id=1, replica_groups=mesh['panel'=2,'colat'=16,'lon'=16] {'lon'}, dimensions={1}, use_global_device_ids=true | all-gather | bytes 139264 | tf_op jit(solution)/shard_map/all_gather | solution.py:97
  74.7 42.9 %all_gather.7 = f32[4,128,128]{2,0,1:T(4,128)S(1)} all-gather(f32[4,8,128]{2,0,1:T(4,128)S(1)} %slice.356), channel_id=1, replica_groups=mesh['panel'=2,'colat'=16,'lon'=16] {'colat'}, dimensions={1}, use_global_device_ids=true | all-gather | bytes 278528 | tf_op jit(solution)/shard_map/all_gather | solution.py:96
  117.6 0.1 copy.57
  117.7 0.1 copy.58
  117.8 0.2 fusion.6
  118.0 0.1 copy.72
  118.1 0.1 copy.59
  118.2 0.1 copy.60
  118.3 0.2 fusion.5
  118.5 1.3 %copy.53 = f32[4,1,16,32,128]{4,3,2,1,0:T(8,128)} copy(f32[4,1,16,32,128]{4,2,3,0,1:T(8,128)S(1)} %fusion.5) | data formatting | bytes 2097152 | tf_op jit(solution)/shard_map/scatter | solution.py:113
  (35 shorter events, 0.3 us)
Async XLA Ops:
  0.0 8.1 %copy-start = (f32[4,1,16,32,128]{4,3,2,1,0:T(8,128)S(1)}, f32[4,1,16,32,128]{4,3,2,1,0:T(8,128)}, u32[]{:S(2)}) copy-start(f32[4,1,16,32,128]{4,3,2,1,0:T(8,128)} %param.19) | copy-start | bytes 3145732
  1.9 6.3 %copy-start.3 = (f32[1,1,1,2,12]{4,3,2,1,0:T(2,128)S(1)}, f32[1,1,1,2,12]{4,3,2,1,0:T(2,128)}, u32[]{:S(2)}) copy-start(f32[1,1,1,2,12]{4,3,2,1,0:T(2,128)} %param.24) | copy-start | bytes 292
  2.0 7.2 %collective-permute-start = (f32[4,2,32,128]{3,1,2,0:T(2,128)S(1)}, f32[4,2,32,128]{3,1,2,0:T(2,128)S(1)}, u32[]{:S(2)}, u32[]{:S(2)}) collective-permute-start(f32[4,2,32,128]{3,1,2,0:T(2,128)S(1)} %get-tuple-element.87), channel_id=1, source_target_pairs={{16,0},{32,16},{48,32},{64,48},{80,64},{96,80},{112,96},{128,112},... | collective-permute-start | bytes 393224 | tf_op jit(solution)/shard_map/ppermute | solution.py:18
  3.3 5.4 %copy-start.1 = (f32[1,16,32,128]{3,2,1,0:T(8,128)S(1)}, f32[1,16,32,128]{3,2,1,0:T(8,128)}, u32[]{:S(2)}) copy-start(f32[1,16,32,128]{3,2,1,0:T(8,128)} %param.20) | copy-start | bytes 786436
  3.4 5.6 %copy-start.2 = (f32[1,16,32,128]{3,2,1,0:T(8,128)S(1)}, f32[1,16,32,128]{3,2,1,0:T(8,128)}, u32[]{:S(2)}) copy-start(f32[1,16,32,128]{3,2,1,0:T(8,128)} %param.21) | copy-start | bytes 786436
  3.4 7.2 %collective-permute-start.1 = (f32[4,2,32,128]{3,1,2,0:T(2,128)S(1)}, f32[4,2,32,128]{3,1,2,0:T(2,128)S(1)}, u32[]{:S(2)}, u32[]{:S(2)}) collective-permute-start(f32[4,2,32,128]{3,1,2,0:T(2,128)S(1)} %get-tuple-element.86), channel_id=1, source_target_pairs={{0,16},{16,32},{32,48},{48,64},{64,80},{80,96},{96,112},{112,128},... | collective-permute-start | bytes 393224 | tf_op jit(solution)/shard_map/ppermute | solution.py:17
  8.2 0.9 copy-start.4
  8.2 0.9 copy-start.5
  8.2 0.9 copy-start.6
  10.6 4.4 %collective-permute-start.2 = (f32[4,20,2,128]{3,1,2,0:T(8,128)S(1)}, f32[4,20,2,128]{3,1,2,0:T(8,128)S(1)}, u32[]{:S(2)}, u32[]{:S(2)}) collective-permute-start(f32[4,20,2,128]{3,1,2,0:T(8,128)S(1)} %get-tuple-element.76), channel_id=1, source_target_pairs={{1,0},{2,1},{3,2},{4,3},{5,4},{6,5},{7,6},{8,7},{9,8},{10,9},{11,1... | collective-permute-start | bytes 245768 | tf_op jit(solution)/shard_map/ppermute | solution.py:18
  12.5 5.9 %collective-permute-start.3 = (f32[4,20,2,128]{3,1,2,0:T(8,128)S(1)}, f32[4,20,2,128]{3,1,2,0:T(8,128)S(1)}, u32[]{:S(2)}, u32[]{:S(2)}) collective-permute-start(f32[4,20,2,128]{3,1,2,0:T(8,128)S(1)} %get-tuple-element.77), channel_id=1, source_target_pairs={{0,1},{1,2},{2,3},{3,4},{4,5},{5,6},{6,7},{7,8},{8,9},{9,10},{10,1... | collective-permute-start | bytes 245768 | tf_op jit(solution)/shard_map/ppermute | solution.py:17
  22.2 6.4 %collective-permute-start.4 = (f32[4,1,32,128]{3,1,2,0:T(1,128)S(1)}, f32[4,1,32,128]{3,1,2,0:T(1,128)S(1)}, u32[]{:S(2)}, u32[]{:S(2)}) collective-permute-start(f32[4,1,32,128]{3,1,2,0:T(1,128)S(1)} %get-tuple-element.80), channel_id=1, source_target_pairs={{0,16},{16,32},{32,48},{48,64},{64,80},{80,96},{96,112},{112,128},... | collective-permute-start | bytes 196616 | tf_op jit(solution)/shard_map/ppermute | solution.py:17
  26.6 6.2 %collective-permute-start.5 = (f32[4,1,32,128]{3,1,2,0:T(1,128)S(1)}, f32[4,1,32,128]{3,1,2,0:T(1,128)S(1)}, u32[]{:S(2)}, u32[]{:S(2)}) collective-permute-start(f32[4,1,32,128]{3,1,2,0:T(1,128)S(1)} %get-tuple-element.81), channel_id=1, source_target_pairs={{16,0},{32,16},{48,32},{64,48},{80,64},{96,80},{112,96},{128,112},... | collective-permute-start | bytes 196616 | tf_op jit(solution)/shard_map/ppermute | solution.py:18
  32.8 5.6 %collective-permute-start.6 = (f32[4,18,1,128]{3,1,2,0:T(8,128)S(1)}, f32[4,18,1,128]{3,1,2,0:T(8,128)S(1)}, u32[]{:S(2)}, u32[]{:S(2)}) collective-permute-start(f32[4,18,1,128]{3,1,2,0:T(8,128)S(1)} %get-tuple-element.78), channel_id=1, source_target_pairs={{0,1},{1,2},{2,3},{3,4},{4,5},{5,6},{6,7},{7,8},{8,9},{9,10},{10,1... | collective-permute-start | bytes 110600 | tf_op jit(solution)/shard_map/ppermute | solution.py:17
  34.7 6.7 %collective-permute-start.7 = (f32[4,18,1,128]{3,1,2,0:T(8,128)S(1)}, f32[4,18,1,128]{3,1,2,0:T(8,128)S(1)}, u32[]{:S(2)}, u32[]{:S(2)}) collective-permute-start(f32[4,18,1,128]{3,1,2,0:T(8,128)S(1)} %get-tuple-element.79), channel_id=1, source_target_pairs={{1,0},{2,1},{3,2},{4,3},{5,4},{6,5},{7,6},{8,7},{9,8},{10,9},{11,1... | collective-permute-start | bytes 110600 | tf_op jit(solution)/shard_map/ppermute | solution.py:18
  44.8 12.7 %collective-permute-start.8 = (f32[4,12,128]{2,0,1:T(4,128)S(1)}, f32[4,12,128]{2,0,1:T(4,128)S(1)}, u32[]{:S(2)}, u32[]{:S(2)}) collective-permute-start(f32[4,12,128]{2,0,1:T(4,128)S(1)} %pad_maximum_fusion.10), channel_id=1, source_target_pairs={{0,256},{256,0},{1,257},{257,1},{2,258},{258,2},{3,259},{259,3},{4... | collective-permute-start | bytes 73736 | tf_op jit(solution)/shard_map/ppermute | solution.py:30
where the time goes:
time: 120 us
  blocking collectives  60 us (50%)
  starting transfers between devices  32.4 us (27%)
  waiting for transfers between devices  14.5 us (12%)
  local copies, waits for them, and re-layouts  7.47 us (6%)
  other arithmetic  4.91 us (4%)
    all_gather x1, blocking collectives, local(): lax.all_gather(arrived[:, 0:row_share], 'colat', axis=1, tiled=True)  42.9 us
    all_gather x1, blocking collectives, local(): col_full = lax.all_gather(arrived[:, row_share:], 'lon', axis=1, tiled=True)  17.1 us
    ppermute x4, starting transfers between devices, with_halo(): before = lax.ppermute(last, axis, up)  13.4 us
    ppermute x1, starting transfers between devices, swapped(): return lax.ppermute(block, axis, route)  10.9 us
    ppermute x4, starting transfers between devices, with_halo(): after = lax.ppermute(leading, axis, down)  8.15 us
    ppermute x4, waiting for transfers between devices, with_halo(): after = lax.ppermute(leading, axis, down)  7.22 us
    ppermute x4, waiting for transfers between devices, with_halo(): before = lax.ppermute(last, axis, up)  5.49 us
    unnamed x22, local copies, waits for them, and re-layouts  2.63 us
  transfers between devices with their start and end apart: 9, of which 6 were waited for; matrix products, arithmetic and copies ran while one was open for 1% of the time, Pallas kernels for 0%

commit v1 on v0

--- a/solution.py
+++ b/solution.py
@@ -93,7 +93,13 @@
     turned_lon = sine_part * blended[2] + cosine * blended[3]
     blended = jnp.stack([blended[0], blended[1], turned_lat, turned_lon])
     arrived = swapped(blended, "panel", 0)
-    row_full = lax.all_gather(arrived[:, 0:row_share], "colat", axis=1, tiled=True)
+    _show_corner = lambda tile_in, axis_name: jnp.concatenate(
+        lax.all_to_all(
+            jnp.stack([tile_in for _ in range(lax.axis_size(axis_name))]), axis_name, 0, 0
+        ),
+        axis=1,
+    )
+    row_full = _show_corner(arrived[:, 0:row_share], "colat")
     col_full = lax.all_gather(arrived[:, row_share:], "lon", axis=1, tiled=True)
     col_blocks = col_full.reshape(4, 4, height, radial_len)
     west_strip = jnp.transpose(

time: 120 us -> 101 us (0.84)
  blocking collectives: 60 us -> 17.1 us
  starting transfers between devices: 32.4 us -> 45 us
  waiting for transfers between devices: 14.5 us -> 25.6 us
    all_gather x1 -> x0, blocking collectives: 42.9 us -> none  [local(): lax.all_gather(arrived[:, 0:row_share], 'colat', axis=1, tiled=True)]
    all_to_all x0 -> x1, starting transfers between devices: none -> 12.5 us  [local(): lax.all_to_all(jnp.stack([tile_in for _ in range(lax.axis_size(axis_name)...]
    all_to_all x0 -> x1, waiting for transfers between devices: none -> 11.1 us  [local(): lax.all_to_all(jnp.stack([tile_in for _ in range(lax.axis_size(axis_name)...]
    unnamed x22 -> x18, local copies, waits for them, and re-layouts: 2.63 us -> 2.35 us
  transfers between devices with their start and end apart: 9 -> 10, of which waited for: 6 -> 7; matrix products, arithmetic and copies ran while one was open for 1% -> 1% of each run, Pallas kernels for 0% -> 0%
where the time goes in v1:
time: 101 us
  starting transfers between devices  45 us (45%)
  waiting for transfers between devices  25.6 us (25%)
  blocking collectives  17.1 us (17%)
  local copies, waits for them, and re-layouts  7.95 us (8%)
  other arithmetic  4.89 us (5%)
    all_gather x1, blocking collectives, local(): col_full = lax.all_gather(arrived[:, row_share:], 'lon', axis=1, tiled=True)  17.1 us
    ppermute x4, starting transfers between devices, with_halo(): before = lax.ppermute(last, axis, up)  13.4 us
    all_to_all x1, starting transfers between devices, local(): lax.all_to_all(jnp.stack([tile_in for _ in range(lax.axis_size(axis_name)...  12.5 us
    all_to_all x1, waiting for transfers between devices, local(): lax.all_to_all(jnp.stack([tile_in for _ in range(lax.axis_size(axis_name)...  11.1 us
    ppermute x1, starting transfers between devices, swapped(): return lax.ppermute(block, axis, route)  10.9 us
    ppermute x4, starting transfers between devices, with_halo(): after = lax.ppermute(leading, axis, down)  8.15 us
    ppermute x4, waiting for transfers between devices, with_halo(): after = lax.ppermute(leading, axis, down)  7.22 us
    ppermute x4, waiting for transfers between devices, with_halo(): before = lax.ppermute(last, axis, up)  5.49 us
  transfers between devices with their start and end apart: 10, of which 7 were waited for; matrix products, arithmetic and copies ran while one was open for 1% of the time, Pallas kernels for 0%

profile of v1, /device:TPU:24, one launch (start us, length us, event | category | flops | bytes accessed | tf_op | source)
XLA Modules:
  0.0 101.0 jit_solution(13431827511904505346)
XLA Ops:
  0.0 1.9 %copy.68 = f32[4,1,16,32,128]{4,2,3,0,1:T(8,128)S(1)} copy(f32[4,1,16,32,128]{4,3,2,1,0:T(8,128)} %param.19) | data formatting | bytes 2097152 | tf_op args[0]
  1.9 0.0 copy-start.3
  1.9 0.1 fusion.16
  2.0 1.3 %collective-permute-start = (f32[4,2,32,128]{3,1,2,0:T(2,128)S(1)}, f32[4,2,32,128]{3,1,2,0:T(2,128)S(1)}, u32[]{:S(2)}, u32[]{:S(2)}) collective-permute-start(f32[4,2,32,128]{3,1,2,0:T(2,128)S(1)} %get-tuple-element.87), channel_id=1, source_target_pairs={{16,0},{32,16},{48,32},{64,48},{80,64},{96,80},{112,96},{128,112},... | collective-permute-start | bytes 393224 | tf_op jit(solution)/shard_map/ppermute | solution.py:18
  3.3 0.0 copy-start.1
  3.4 0.0 copy-start.2
  3.4 4.7 %collective-permute-start.1 = (f32[4,2,32,128]{3,1,2,0:T(2,128)S(1)}, f32[4,2,32,128]{3,1,2,0:T(2,128)S(1)}, u32[]{:S(2)}, u32[]{:S(2)}) collective-permute-start(f32[4,2,32,128]{3,1,2,0:T(2,128)S(1)} %get-tuple-element.86), channel_id=1, source_target_pairs={{0,16},{16,32},{32,48},{48,64},{64,80},{80,96},{96,112},{112,128},... | collective-permute-start | bytes 393224 | tf_op jit(solution)/shard_map/ppermute | solution.py:17
  8.1 0.1 fusion.15
  8.2 0.0 copy-start.4
  8.3 0.2 copy.44
  8.4 0.2 copy.45
  8.6 0.2 copy.46
  8.8 0.2 copy.40
  9.0 0.2 copy.41
  9.2 1.3 %collective-permute-done.1 = f32[4,2,32,128]{3,1,2,0:T(2,128)S(1)} collective-permute-done((f32[4,2,32,128]{3,1,2,0:T(2,128)S(1)}, f32[4,2,32,128]{3,1,2,0:T(2,128)S(1)}, u32[]{:S(2)}, u32[]{:S(2)}) %collective-permute-start.1) | collective-permute-done | bytes 131104 | tf_op jit(solution)/shard_map/ppermute | solution.py:17
  10.6 1.9 %collective-permute-start.2 = (f32[4,20,2,128]{3,1,2,0:T(8,128)S(1)}, f32[4,20,2,128]{3,1,2,0:T(8,128)S(1)}, u32[]{:S(2)}, u32[]{:S(2)}) collective-permute-start(f32[4,20,2,128]{3,1,2,0:T(8,128)S(1)} %get-tuple-element.76), channel_id=1, source_target_pairs={{1,0},{2,1},{3,2},{4,3},{5,4},{6,5},{7,6},{8,7},{9,8},{10,9},{11,1... | collective-permute-start | bytes 245768 | tf_op jit(solution)/shard_map/ppermute | solution.py:18
  12.5 2.4 %collective-permute-start.3 = (f32[4,20,2,128]{3,1,2,0:T(8,128)S(1)}, f32[4,20,2,128]{3,1,2,0:T(8,128)S(1)}, u32[]{:S(2)}, u32[]{:S(2)}) collective-permute-start(f32[4,20,2,128]{3,1,2,0:T(8,128)S(1)} %get-tuple-element.77), channel_id=1, source_target_pairs={{0,1},{1,2},{2,3},{3,4},{4,5},{5,6},{6,7},{7,8},{8,9},{9,10},{10,1... | collective-permute-start | bytes 245768 | tf_op jit(solution)/shard_map/ppermute | solution.py:17
  15.0 3.5 %collective-permute-done.3 = f32[4,20,2,128]{3,1,2,0:T(8,128)S(1)} collective-permute-done((f32[4,20,2,128]{3,1,2,0:T(8,128)S(1)}, f32[4,20,2,128]{3,1,2,0:T(8,128)S(1)}, u32[]{:S(2)}, u32[]{:S(2)}) %collective-permute-start.3) | collective-permute-done | bytes 81952 | tf_op jit(solution)/shard_map/ppermute | solution.py:17
  18.5 0.3 pad_maximum_fusion
  18.7 2.5 %fusion.2 = f32[4,16,32,128]{3,1,2,0:T(8,128)S(1)} fusion(f32[1,16,32,128]{3,1,2,0:T(8,128)S(1)} %copy.41, f32[1,16,32,128]{3,1,2,0:T(8,128)S(1)} %copy.40, f32[4,20,34,128]{3,1,2,0:T(8,128)S(1)} %get-tuple-element.75, f32[4,20,34,128]{3,1,2,0:T(8,128)S(1)} %get-tuple-element.74, f32[4,2,32,128]{3,1,2,0:T(2,128)S(1)} %collective-permute-done, ...), kind=kLoop, calls=%fused_computation.20 | loop fusion | flops 11796480 | bytes 7864320 | tf_op jit(solution)/shard_map/sub | solution.py:57
  21.2 0.2 fusion.3
  21.5 0.7 multiply_add_fusion
  22.1 0.1 fusion.14
  22.2 4.4 %collective-permute-start.4 = (f32[4,1,32,128]{3,1,2,0:T(1,128)S(1)}, f32[4,1,32,128]{3,1,2,0:T(1,128)S(1)}, u32[]{:S(2)}, u32[]{:S(2)}) collective-permute-start(f32[4,1,32,128]{3,1,2,0:T(1,128)S(1)} %get-tuple-element.80), channel_id=1, source_target_pairs={{0,16},{16,32},{32,48},{48,64},{64,80},{80,96},{96,112},{112,128},... | collective-permute-start | bytes 196616 | tf_op jit(solution)/shard_map/ppermute | solution.py:17
  26.6 1.3 %collective-permute-start.5 = (f32[4,1,32,128]{3,1,2,0:T(1,128)S(1)}, f32[4,1,32,128]{3,1,2,0:T(1,128)S(1)}, u32[]{:S(2)}, u32[]{:S(2)}) collective-permute-start(f32[4,1,32,128]{3,1,2,0:T(1,128)S(1)} %get-tuple-element.81), channel_id=1, source_target_pairs={{16,0},{32,16},{48,32},{64,48},{80,64},{96,80},{112,96},{128,112},... | collective-permute-start | bytes 196616 | tf_op jit(solution)/shard_map/ppermute | solution.py:18
  27.9 0.7 collective-permute-done.4
  28.6 4.2 %collective-permute-done.5 = f32[4,1,32,128]{3,1,2,0:T(1,128)S(1)} collective-permute-done((f32[4,1,32,128]{3,1,2,0:T(1,128)S(1)}, f32[4,1,32,128]{3,1,2,0:T(1,128)S(1)}, u32[]{:S(2)}, u32[]{:S(2)}) %collective-permute-start.5) | collective-permute-done | bytes 65568 | tf_op jit(solution)/shard_map/ppermute | solution.py:18
  32.8 1.9 %collective-permute-start.6 = (f32[4,18,1,128]{3,1,2,0:T(8,128)S(1)}, f32[4,18,1,128]{3,1,2,0:T(8,128)S(1)}, u32[]{:S(2)}, u32[]{:S(2)}) collective-permute-start(f32[4,18,1,128]{3,1,2,0:T(8,128)S(1)} %get-tuple-element.78), channel_id=1, source_target_pairs={{0,1},{1,2},{2,3},{3,4},{4,5},{5,6},{6,7},{7,8},{8,9},{9,10},{10,1... | collective-permute-start | bytes 110600 | tf_op jit(solution)/shard_map/ppermute | solution.py:17
  34.7 3.6 %collective-permute-start.7 = (f32[4,18,1,128]{3,1,2,0:T(8,128)S(1)}, f32[4,18,1,128]{3,1,2,0:T(8,128)S(1)}, u32[]{:S(2)}, u32[]{:S(2)}) collective-permute-start(f32[4,18,1,128]{3,1,2,0:T(8,128)S(1)} %get-tuple-element.79), channel_id=1, source_target_pairs={{1,0},{2,1},{3,2},{4,3},{5,4},{6,5},{7,6},{8,7},{9,8},{10,9},{11,1... | collective-permute-start | bytes 110600 | tf_op jit(solution)/shard_map/ppermute | solution.py:18
  38.4 3.1 %collective-permute-done.7 = f32[4,18,1,128]{3,1,2,0:T(8,128)S(1)} collective-permute-done((f32[4,18,1,128]{3,1,2,0:T(8,128)S(1)}, f32[4,18,1,128]{3,1,2,0:T(8,128)S(1)}, u32[]{:S(2)}, u32[]{:S(2)}) %collective-permute-start.7) | collective-permute-done | bytes 36896 | tf_op jit(solution)/shard_map/ppermute | solution.py:18
  41.4 0.3 pad_maximum_fusion.1
  41.7 0.5 copy.48
  42.2 0.6 gather_fusion.2
  42.8 0.6 gather_fusion.3
  43.4 0.6 gather_fusion.1
  43.9 0.6 gather_fusion
  44.5 0.2 fusion.11
  44.7 0.1 multiply_subtract_fusion
  44.8 10.9 %collective-permute-start.8 = (f32[4,12,128]{2,0,1:T(4,128)S(1)}, f32[4,12,128]{2,0,1:T(4,128)S(1)}, u32[]{:S(2)}, u32[]{:S(2)}) collective-permute-start(f32[4,12,128]{2,0,1:T(4,128)S(1)} %pad_maximum_fusion.10), channel_id=1, source_target_pairs={{0,256},{256,0},{1,257},{257,1},{2,258},{258,2},{3,259},{259,3},{4... | collective-permute-start | bytes 73736 | tf_op jit(solution)/shard_map/ppermute | solution.py:30
  55.8 1.8 %collective-permute-done.8 = f32[4,12,128]{2,0,1:T(4,128)S(1)} collective-permute-done((f32[4,12,128]{2,0,1:T(4,128)S(1)}, f32[4,12,128]{2,0,1:T(4,128)S(1)}, u32[]{:S(2)}, u32[]{:S(2)}) %collective-permute-start.8) | collective-permute-done | bytes 24608 | tf_op jit(solution)/shard_map/ppermute | solution.py:30
  57.6 17.1 %all_gather.3 = f32[4,64,128]{2,0,1:T(4,128)S(1)} all-gather(f32[4,4,128]{2,0,1:T(4,128)S(1)} %slice.349), channel_id=1, replica_groups=mesh['panel'=2,'colat'=16,'lon'=16] {'lon'}, dimensions={1}, use_global_device_ids=true | all-gather | bytes 139264 | tf_op jit(solution)/shard_map/all_gather | solution.py:103
  74.7 0.7 stack.19
  75.4 12.5 %all-to-all-start = ((f32[16,4,8,128]{3,2,1,0:T(8,128)}), f32[16,4,8,128]{3,2,1,0:T(8,128)S(1)}, u32[]{:S(2)}, u32[]{:S(2)}) async-start(f32[16,4,8,128]{3,2,1,0:T(8,128)} %stack.19), calls=%async_computation | async-start | bytes 524288 | tf_op jit(solution)/shard_map/all_to_all | solution.py:97
  88.0 11.1 %all-to-all-done = f32[16,4,8,128]{3,2,1,0:T(8,128)S(1)} async-done(((f32[16,4,8,128]{3,2,1,0:T(8,128)}), f32[16,4,8,128]{3,2,1,0:T(8,128)S(1)}, u32[]{:S(2)}, u32[]{:S(2)}) %all-to-all-start) | async-done | bytes 262176 | tf_op jit(solution)/shard_map/all_to_all | solution.py:97
  99.2 0.2 fusion.6
  99.4 0.1 copy.73
  99.5 0.2 fusion.5
  99.7 1.3 %copy.56 = f32[4,1,16,32,128]{4,3,2,1,0:T(8,128)} copy(f32[4,1,16,32,128]{4,2,3,0,1:T(8,128)S(1)} %fusion.5) | data formatting | bytes 2097152 | tf_op jit(solution)/shard_map/scatter | solution.py:119
  (35 shorter events, 0.3 us)
Async XLA Ops:
  0.0 8.1 %copy-start = (f32[4,1,16,32,128]{4,3,2,1,0:T(8,128)S(1)}, f32[4,1,16,32,128]{4,3,2,1,0:T(8,128)}, u32[]{:S(2)}) copy-start(f32[4,1,16,32,128]{4,3,2,1,0:T(8,128)} %param.19) | copy-start | bytes 3145732
  1.9 6.3 %copy-start.3 = (f32[1,1,1,2,12]{4,3,2,1,0:T(2,128)S(1)}, f32[1,1,1,2,12]{4,3,2,1,0:T(2,128)}, u32[]{:S(2)}) copy-start(f32[1,1,1,2,12]{4,3,2,1,0:T(2,128)} %param.24) | copy-start | bytes 292
  2.0 7.2 %collective-permute-start = (f32[4,2,32,128]{3,1,2,0:T(2,128)S(1)}, f32[4,2,32,128]{3,1,2,0:T(2,128)S(1)}, u32[]{:S(2)}, u32[]{:S(2)}) collective-permute-start(f32[4,2,32,128]{3,1,2,0:T(2,128)S(1)} %get-tuple-element.87), channel_id=1, source_target_pairs={{16,0},{32,16},{48,32},{64,48},{80,64},{96,80},{112,96},{128,112},... | collective-permute-start | bytes 393224 | tf_op jit(solution)/shard_map/ppermute | solution.py:18
  3.3 5.4 %copy-start.1 = (f32[1,16,32,128]{3,2,1,0:T(8,128)S(1)}, f32[1,16,32,128]{3,2,1,0:T(8,128)}, u32[]{:S(2)}) copy-start(f32[1,16,32,128]{3,2,1,0:T(8,128)} %param.20) | copy-start | bytes 786436
  3.4 5.6 %copy-start.2 = (f32[1,16,32,128]{3,2,1,0:T(8,128)S(1)}, f32[1,16,32,128]{3,2,1,0:T(8,128)}, u32[]{:S(2)}) copy-start(f32[1,16,32,128]{3,2,1,0:T(8,128)} %param.21) | copy-start | bytes 786436
  3.4 7.2 %collective-permute-start.1 = (f32[4,2,32,128]{3,1,2,0:T(2,128)S(1)}, f32[4,2,32,128]{3,1,2,0:T(2,128)S(1)}, u32[]{:S(2)}, u32[]{:S(2)}) collective-permute-start(f32[4,2,32,128]{3,1,2,0:T(2,128)S(1)} %get-tuple-element.86), channel_id=1, source_target_pairs={{0,16},{16,32},{32,48},{48,64},{64,80},{80,96},{96,112},{112,128},... | collective-permute-start | bytes 393224 | tf_op jit(solution)/shard_map/ppermute | solution.py:17
  8.2 0.9 copy-start.4
  8.2 0.9 copy-start.5
  8.2 0.9 copy-start.6
  10.6 4.4 %collective-permute-start.2 = (f32[4,20,2,128]{3,1,2,0:T(8,128)S(1)}, f32[4,20,2,128]{3,1,2,0:T(8,128)S(1)}, u32[]{:S(2)}, u32[]{:S(2)}) collective-permute-start(f32[4,20,2,128]{3,1,2,0:T(8,128)S(1)} %get-tuple-element.76), channel_id=1, source_target_pairs={{1,0},{2,1},{3,2},{4,3},{5,4},{6,5},{7,6},{8,7},{9,8},{10,9},{11,1... | collective-permute-start | bytes 245768 | tf_op jit(solution)/shard_map/ppermute | solution.py:18
  12.5 5.9 %collective-permute-start.3 = (f32[4,20,2,128]{3,1,2,0:T(8,128)S(1)}, f32[4,20,2,128]{3,1,2,0:T(8,128)S(1)}, u32[]{:S(2)}, u32[]{:S(2)}) collective-permute-start(f32[4,20,2,128]{3,1,2,0:T(8,128)S(1)} %get-tuple-element.77), channel_id=1, source_target_pairs={{0,1},{1,2},{2,3},{3,4},{4,5},{5,6},{6,7},{7,8},{8,9},{9,10},{10,1... | collective-permute-start | bytes 245768 | tf_op jit(solution)/shard_map/ppermute | solution.py:17
  22.2 6.4 %collective-permute-start.4 = (f32[4,1,32,128]{3,1,2,0:T(1,128)S(1)}, f32[4,1,32,128]{3,1,2,0:T(1,128)S(1)}, u32[]{:S(2)}, u32[]{:S(2)}) collective-permute-start(f32[4,1,32,128]{3,1,2,0:T(1,128)S(1)} %get-tuple-element.80), channel_id=1, source_target_pairs={{0,16},{16,32},{32,48},{48,64},{64,80},{80,96},{96,112},{112,128},... | collective-permute-start | bytes 196616 | tf_op jit(solution)/shard_map/ppermute | solution.py:17
  26.6 6.2 %collective-permute-start.5 = (f32[4,1,32,128]{3,1,2,0:T(1,128)S(1)}, f32[4,1,32,128]{3,1,2,0:T(1,128)S(1)}, u32[]{:S(2)}, u32[]{:S(2)}) collective-permute-start(f32[4,1,32,128]{3,1,2,0:T(1,128)S(1)} %get-tuple-element.81), channel_id=1, source_target_pairs={{16,0},{32,16},{48,32},{64,48},{80,64},{96,80},{112,96},{128,112},... | collective-permute-start | bytes 196616 | tf_op jit(solution)/shard_map/ppermute | solution.py:18
  32.8 5.6 %collective-permute-start.6 = (f32[4,18,1,128]{3,1,2,0:T(8,128)S(1)}, f32[4,18,1,128]{3,1,2,0:T(8,128)S(1)}, u32[]{:S(2)}, u32[]{:S(2)}) collective-permute-start(f32[4,18,1,128]{3,1,2,0:T(8,128)S(1)} %get-tuple-element.78), channel_id=1, source_target_pairs={{0,1},{1,2},{2,3},{3,4},{4,5},{5,6},{6,7},{7,8},{8,9},{9,10},{10,1... | collective-permute-start | bytes 110600 | tf_op jit(solution)/shard_map/ppermute | solution.py:17
  34.7 6.7 %collective-permute-start.7 = (f32[4,18,1,128]{3,1,2,0:T(8,128)S(1)}, f32[4,18,1,128]{3,1,2,0:T(8,128)S(1)}, u32[]{:S(2)}, u32[]{:S(2)}) collective-permute-start(f32[4,18,1,128]{3,1,2,0:T(8,128)S(1)} %get-tuple-element.79), channel_id=1, source_target_pairs={{1,0},{2,1},{3,2},{4,3},{5,4},{6,5},{7,6},{8,7},{9,8},{10,9},{11,1... | collective-permute-start | bytes 110600 | tf_op jit(solution)/shard_map/ppermute | solution.py:18
  44.8 12.7 %collective-permute-start.8 = (f32[4,12,128]{2,0,1:T(4,128)S(1)}, f32[4,12,128]{2,0,1:T(4,128)S(1)}, u32[]{:S(2)}, u32[]{:S(2)}) collective-permute-start(f32[4,12,128]{2,0,1:T(4,128)S(1)} %pad_maximum_fusion.10), channel_id=1, source_target_pairs={{0,256},{256,0},{1,257},{257,1},{2,258},{258,2},{3,259},{259,3},{4... | collective-permute-start | bytes 73736 | tf_op jit(solution)/shard_map/ppermute | solution.py:30
  75.4 23.7 %all-to-all-start = ((f32[16,4,8,128]{3,2,1,0:T(8,128)}), f32[16,4,8,128]{3,2,1,0:T(8,128)S(1)}, u32[]{:S(2)}, u32[]{:S(2)}) async-start(f32[16,4,8,128]{3,2,1,0:T(8,128)} %stack.19), calls=%async_computation | async-start | bytes 524288 | tf_op jit(solution)/shard_map/all_to_all | solution.py:97
